TPU v7x, 32 devices: a whole 2x2x4 slice. The times are simulated.
32 devices in a mesh: row: 2 (over y), col: 4 (over x, core), tm: 4 (over z).
Axes of the slice: x: 2, y: 2, z: 4, core: 2. Of those that a mesh axis runs over, the one named last changes fastest.
Arguments:
- filled_orbitals: bfloat16 [4, 1024, 1024], P('col', 'row', 'tm'), may hold values from -0.1875 to 0.1875
- empty_orbitals: bfloat16 [4, 1024, 3072], P('col', 'row', 'tm'), may hold values from -0.109375 to 0.109375
- filled_depth: bfloat16 [1024], P('tm'), may hold values from 0.019897461 to 2
- empty_depth: bfloat16 [3072], P('tm'), may hold values from 0.019897461 to 2
- time_points: float32 [4], P('tm'), may hold values from 0.05 to 8
- cosine_weights: float32 [4, 4], replicated, may hold values from -3 to 3
Outputs:
- polar_freq: float32 [4, 4, 1024, 4096], P(None, None, ('row', 'tm'), 'col')
All inputs are finite; a program needn't handle non-finite values.
Results may differ from a plain program's by a relative error of at most 0.0033.
Values may be sent and summed in bfloat16 or wider, within the bound.
No kernel may reach another device: no remote copies, remote signals or barrier semaphores. Data moves between devices by JAX's collectives and lax.ppermute only.
A program may use at most 128 MiB of HBM per device.

v0:
```python
import jax
import jax.numpy as jnp
from jax import lax
from jax.sharding import PartitionSpec as P


def tile_product(left_points, right_points, depths, tau_value):
    band_count = left_points.shape[-1]
    weight_row = jnp.exp(-depths.astype(jnp.float32) * tau_value)
    scaled = (
        right_points.reshape(-1, band_count).astype(jnp.float32) * weight_row[None, :]
    ).astype(jnp.bfloat16)
    return lax.dot_general(
        left_points.reshape(-1, band_count),
        scaled,
        (((1,), (1,)), ((), ())),
        preferred_element_type=jnp.float32,
    )


def on_device(
    filled_orbitals, empty_orbitals, filled_depth, empty_depth, time_points, cosine_weights
):
    tau_value = time_points[0]
    filled_bands, empty_bands, filled_all, empty_all = (
        lax.all_gather(filled_orbitals, "tm", axis=2, tiled=True),
        lax.all_gather(empty_orbitals, "tm", axis=2, tiled=True),
        lax.all_gather(filled_depth, "tm", axis=0, tiled=True),
        lax.all_gather(empty_depth, "tm", axis=0, tiled=True),
    )
    filled_rows, empty_rows = (
        lax.all_gather(filled_bands, "col", axis=0, tiled=True),
        lax.all_gather(empty_bands, "col", axis=0, tiled=True),
    )
    column_filled, column_empty = lax.all_gather(
        (filled_bands, empty_bands), "row", axis=1, tiled=True
    )
    green_filled = tile_product(filled_rows, column_filled, filled_all, tau_value)
    green_empty = tile_product(empty_rows, column_empty, empty_all, tau_value)
    polar_time = (
        (-(green_filled * green_empty))
        .astype(jnp.bfloat16)
        .reshape(filled_rows.shape[0], filled_rows.shape[1], -1)
    )
    return jnp.einsum(
        "ft,tabc->fabc",
        cosine_weights,
        lax.all_to_all(polar_time[None], "tm", split_axis=2, concat_axis=0, tiled=True).astype(
            jnp.float32
        ),
        precision=lax.Precision.HIGHEST,
    )


def solution(mesh):
    in_specs = (P("col", "row", "tm"), P("col", "row", "tm"), P("tm"), P("tm"), P("tm"), P())
    out_specs = P(None, None, ("row", "tm"), "col")
    return jax.shard_map(
        on_device, mesh=mesh, in_specs=in_specs, out_specs=out_specs, check_vma=False
    )
```

profile of v0, /device:TPU:0, one launch (start us, length us, event | category | flops | bytes accessed | tf_op | source)
XLA Modules:
  0.0 491.7 jit_solution(13205183618008928850)
XLA Ops:
  6.5 0.0 copy-start
  6.5 0.0 all-gather.15.cloned.1.call-start
  6.5 0.7 all-gather.15.cloned.1.call-update
  7.3 0.0 all-gather.9.cloned.1.call-start
  7.3 0.7 all-gather.9.cloned.1.call-update
  8.0 0.0 all-gather.17.cloned.1.call-start
  8.1 67.0 %all-gather.15.cloned.1.call-done = bf16[1,512,3072]{2,1,0:T(8,128)(2,1)} async-done(((bf16[1,512,768]{2,1,0:T(8,128)(2,1)}), bf16[1,512,3072]{2,1,0:T(8,128)(2,1)}) %all-gather.15.cloned.1.call-update) | async-done | bytes 3145744 | tf_op jit(solution)/shard_map/all_gather | solution.py:27
  75.1 0.0 copy-start.1
  75.1 0.0 copy-start.2
  75.1 0.0 all-gather.17.cloned.1.call-update
  75.1 0.0 all-gather.19.cloned.1.call-start
  75.2 0.5 all-gather.19.cloned.1.call-update
  75.7 0.0 all-gather.11.cloned.1.call-start
  75.8 29.5 %all-gather.9.cloned.1.call-done = bf16[1,512,1024]{2,1,0:T(8,128)(2,1)} async-done(((bf16[1,512,256]{2,1,0:T(8,128)(2,1)}), bf16[1,512,1024]{2,1,0:T(8,128)(2,1)}) %all-gather.9.cloned.1.call-update) | async-done | bytes 1048592 | tf_op jit(solution)/shard_map/all_gather | solution.py:26
  105.3 0.0 all-gather.11.cloned.1.call-update
  105.3 0.0 all-gather.13.cloned.1.call-start
  105.3 0.5 all-gather.13.cloned.1.call-update
  106.5 0.0 copy-done.1
  106.5 0.0 copy-done.2
  106.6 10.1 %all-gather = bf16[4,1,256]{2,1,0:T(2,128)(2,1)S(1)} all-gather(bf16[1,1,256]{2,1,0:T(2,128)(2,1)S(1)} %reshape.26), channel_id=1, replica_groups=mesh['row'=2,'col'=4,'tm'=4] {'tm'}, dimensions={0}, use_global_device_ids=true | all-gather | bytes 2560 | tf_op jit(solution)/shard_map/all_gather | solution.py:28
  116.7 13.1 %all-gather.1 = bf16[4,1,768]{2,1,0:T(2,128)(2,1)S(1)} all-gather(bf16[1,1,768]{2,1,0:T(2,128)(2,1)S(1)} %reshape.28), channel_id=1, replica_groups=mesh['row'=2,'col'=4,'tm'=4] {'tm'}, dimensions={0}, use_global_device_ids=true | all-gather | bytes 7680 | tf_op jit(solution)/shard_map/all_gather | solution.py:29
  129.8 55.7 %all-gather.17.cloned.1.call-done = bf16[1,1024,3072]{2,1,0:T(8,128)(2,1)} async-done(((bf16[1,512,3072]{2,1,0:T(8,128)(2,1)}), bf16[1,1024,3072]{2,1,0:T(8,128)(2,1)}) %all-gather.17.cloned.1.call-update) | async-done | bytes 6291472 | tf_op jit(solution)/shard_map/all_gather | solution.py:35
  185.5 83.5 %all-gather.19.cloned.1.call-done = bf16[4,512,3072]{2,1,0:T(8,128)(2,1)} async-done(((bf16[1,512,3072]{2,1,0:T(8,128)(2,1)}), bf16[4,512,3072]{2,1,0:T(8,128)(2,1)}) %all-gather.19.cloned.1.call-update) | async-done | bytes 12582928 | tf_op jit(solution)/shard_map/all_gather | solution.py:33
  269.0 18.9 %fusion.1 = f32[1024,2048]{1,0:T(8,128)} fusion(bf16[2048,3072]{1,0:T(8,128)(2,1)} %bitcast.35, bf16[1,1024,3072]{2,1,0:T(8,128)(2,1)} %all-gather.17.cloned.1.call-done, f32[3072]{0:T(1024)S(1)} %bitcast.33), kind=kOutput, calls=%fused_computation.3 | convolution fusion | flops 12894339072 | bytes 27275264 | tf_op jit(solution)/shard_map/dot_general | solution.py:13
  287.9 15.6 %all-gather.11.cloned.1.call-done = bf16[1,1024,1024]{2,1,0:T(8,128)(2,1)} async-done(((bf16[1,512,1024]{2,1,0:T(8,128)(2,1)}), bf16[1,1024,1024]{2,1,0:T(8,128)(2,1)}) %all-gather.11.cloned.1.call-update) | async-done | bytes 2097168 | tf_op jit(solution)/shard_map/all_gather | solution.py:35
  303.5 35.9 %all-gather.13.cloned.1.call-done = bf16[4,512,1024]{2,1,0:T(8,128)(2,1)} async-done(((bf16[1,512,1024]{2,1,0:T(8,128)(2,1)}), bf16[4,512,1024]{2,1,0:T(8,128)(2,1)}) %all-gather.13.cloned.1.call-update) | async-done | bytes 4194320 | tf_op jit(solution)/shard_map/all_gather | solution.py:32
  339.4 11.8 %fusion.6 = bf16[2048,1024]{0,1:T(8,128)(2,1)} fusion(f32[1024,2048]{1,0:T(8,128)} %fusion.1, bf16[2048,1024]{1,0:T(8,128)(2,1)} %bitcast.36, bf16[1,1024,1024]{2,1,0:T(8,128)(2,1)} %all-gather.11.cloned.1.call-done, f32[1024]{0:T(1024)S(1)} %bitcast.34), kind=kOutput, calls=%fused_computation.9 | convolution fusion | flops 4304404480 | bytes 18878464 | tf_op jit(solution)/shard_map/dot_general | solution.py:13
  351.2 7.8 %broadcast_in_dim_reshape.3 = bf16[1,4,512,1024]{2,1,3,0:T(4,128)(2,1)} reshape(bf16[2048,1024]{0,1:T(8,128)(2,1)} %fusion.6) | data formatting | bytes 8388608 | tf_op jit(solution)/shard_map/broadcast_in_dim;reshape | solution.py:48
  359.0 10.0 %copy.11 = bf16[1,4,512,1024]{3,1,0,2:T(4,128)(2,1)} copy(bf16[1,4,512,1024]{2,1,3,0:T(4,128)(2,1)} %broadcast_in_dim_reshape.3) | data formatting | bytes 8388608 | tf_op jit(solution)/shard_map/broadcast_in_dim;reshape | solution.py:48
  369.0 98.1 %all_to_all.18 = bf16[1,4,512,1024]{3,1,0,2:T(4,128)(2,1)S(1)} all-to-all(bf16[1,4,512,1024]{3,1,0,2:T(4,128)(2,1)} %copy.11), channel_id=1, replica_groups=mesh['row'=2,'col'=4,'tm'=4] {'tm'}, dimensions={2} | all-to-all | bytes 8388608 | tf_op jit(solution)/shard_map/all_to_all | solution.py:48
  467.2 0.0 copy-done
  467.2 9.4 %convolution_bitcast_fusion = f32[4,4,128,1024]{3,0,2,1:T(4,128)S(1)} fusion(bf16[1,4,4,128,1024]{4,1,3,2,0:T(4,128)(2,1)S(1)} %bitcast.32, f32[4,4]{1,0:T(4,128)S(1)} %copy-done), kind=kOutput, calls=%fused_computation.5 | convolution fusion | flops 100663296 | bytes 12582976 | tf_op jit(solution)/shard_map/ft,tabc->fabc/dot_general | solution.py:45
  476.6 8.3 %copy.14 = f32[4,4,128,1024]{3,2,1,0:T(8,128)} copy(f32[4,4,128,1024]{3,0,2,1:T(4,128)S(1)} %convolution_bitcast_fusion) | data formatting | bytes 16777216 | tf_op jit(solution)/shard_map/ft,tabc->fabc/dot_general | solution.py:45
  (4 shorter events, 0.1 us)
Async XLA Ops:
  6.5 460.6 %copy-start = (f32[4,4]{1,0:T(4,128)S(1)}, f32[4,4]{1,0:T(4,128)}, u32[]{:S(2)}) copy-start(f32[4,4]{1,0:T(4,128)} %param.11) | copy-start | bytes 196
  6.5 68.6 %all-gather.15.cloned.1.call-start = ((), (), s32[]{:S(2)}) async-start(), calls=%async_computation.4 | async-start | bytes 3932160 | tf_op jit(solution)/shard_map/all_gather | solution.py:27
  7.3 98.0 %all-gather.9.cloned.1.call-start = ((), (), s32[]{:S(2)}) async-start(), calls=%async_computation.1 | async-start | bytes 1310720 | tf_op jit(solution)/shard_map/all_gather | solution.py:26
  8.0 177.5 %all-gather.17.cloned.1.call-start = ((), (), s32[]{:S(2)}) async-start(), calls=%async_computation.5 | async-start | bytes 9437184 | tf_op jit(solution)/shard_map/all_gather | solution.py:35
  75.1 31.4 %copy-start.1 = (bf16[768]{0:T(1024)(128)(2,1)S(1)}, bf16[768]{0:T(1024)(128)(2,1)}, u32[]{:S(2)}) copy-start(bf16[768]{0:T(1024)(128)(2,1)} %param.9) | copy-start | bytes 4612
  75.1 31.4 %copy-start.2 = (bf16[256]{0:T(256)(128)(2,1)S(1)}, bf16[256]{0:T(256)(128)(2,1)}, u32[]{:S(2)}) copy-start(bf16[256]{0:T(256)(128)(2,1)} %param.8) | copy-start | bytes 1540
  75.1 193.9 %all-gather.19.cloned.1.call-start = ((), (), s32[]{:S(2)}) async-start(), calls=%async_computation.6 | async-start | bytes 15728640 | tf_op jit(solution)/shard_map/all_gather | solution.py:33
  75.7 227.8 %all-gather.11.cloned.1.call-start = ((), (), s32[]{:S(2)}) async-start(), calls=%async_computation.2 | async-start | bytes 3145728 | tf_op jit(solution)/shard_map/all_gather | solution.py:35
  105.3 234.2 %all-gather.13.cloned.1.call-start = ((), (), s32[]{:S(2)}) async-start(), calls=%async_computation.3 | async-start | bytes 5242880 | tf_op jit(solution)/shard_map/all_gather | solution.py:32
Sparse Core Ops, SparseCore 0:
  8.9 66.1 all-gather.14
  76.7 28.5 all-gather.8
  106.8 78.6 all-gather.16
  186.9 82.0 all-gather.18
  270.4 33.0 all-gather.10
  305.0 34.4 all-gather.12
where the time goes:
time: 492 us
  waiting for transfers between devices  290 us (59%)
  blocking collectives  121 us (25%)
  matrix products  40.1 us (8%)
  local copies, waits for them, and re-layouts  26.1 us (5%)
  between operations  14.2 us (3%)
    all_to_all x1, blocking collectives, on_device(): lax.all_to_all(polar_time[None], 'tm', split_axis=2, concat_axis=0, tiled...  98.1 us
    all_gather x1, waiting for transfers between devices, on_device(): lax.all_gather(empty_bands, 'col', axis=0, tiled=True)  83.5 us
    all_gather x2, waiting for transfers between devices, on_device(): lax.all_gather((filled_bands, empty_bands), 'row', axis=1, tiled=True)  71.3 us
    all_gather x1, waiting for transfers between devices, on_device(): lax.all_gather(empty_orbitals, 'tm', axis=2, tiled=True)  67 us
    all_gather x1, waiting for transfers between devices, on_device(): lax.all_gather(filled_bands, 'col', axis=0, tiled=True)  35.9 us
    dot_general x2, matrix products, tile_product(): lax.dot_general(left_points.reshape(-1, band_count), scaled, (((1,), (1,)...  30.6 us
    all_gather x1, waiting for transfers between devices, on_device(): lax.all_gather(filled_orbitals, 'tm', axis=2, tiled=True)  29.5 us
    another operation x2, local copies, waits for them, and re-layouts, on_device(): polar_time[None]  17.8 us
  transfers between devices with their start and end apart: 6, of which 6 were waited for; matrix products, arithmetic and copies ran while one was open for 4% of the time, Pallas kernels for 0%

commit v1 on v0

--- a/solution.py
+++ b/solution.py
@@ -2,6 +2,28 @@
 import jax.numpy as jnp
 from jax import lax
 from jax.sharding import PartitionSpec as P
+
+
+def laid_out(blocks, dim):
+    shape = list(blocks.shape[1:])
+    shape[dim] *= blocks.shape[0]
+    return jnp.moveaxis(blocks, 0, dim).reshape(shape)
+
+
+def collected_by_bits(shard, axis):
+    count = lax.axis_size(axis)
+    tiles = shard[None]
+    for level in range(count.bit_length() - 1):
+        apart = 1 << level
+        other = lax.ppermute(tiles, axis, [(i, i ^ apart) for i in range(count)])
+        both = jnp.stack([tiles, other])
+        upper = lax.axis_index(axis) >> level & 1
+        tiles = jnp.where(upper == 0, both, both[::-1]).reshape(-1, *shard.shape)
+    return tiles
+
+
+def gather_by_bits(x, axis, dim):
+    return laid_out(collected_by_bits(x, axis), dim)
 
 
 def tile_product(left_points, right_points, depths, tau_value):
@@ -30,7 +52,7 @@
     )
     filled_rows, empty_rows = (
         lax.all_gather(filled_bands, "col", axis=0, tiled=True),
-        lax.all_gather(empty_bands, "col", axis=0, tiled=True),
+        gather_by_bits(empty_bands, "col", 0),
     )
     column_filled, column_empty = lax.all_gather(
         (filled_bands, empty_bands), "row", axis=1, tiled=True

time: 492 us -> 457 us (0.929)
  waiting for transfers between devices: 290 us -> 228 us
  other arithmetic: 0.04 us -> 23.7 us
    all_gather x1 -> x0, waiting for transfers between devices: 83.5 us -> none  [on_device(): lax.all_gather(empty_bands, 'col', axis=0, tiled=True)]
    ppermute x0 -> x2, waiting for transfers between devices: none -> 80.8 us  [collected_by_bits(): other = lax.ppermute(tiles, axis, [(i, i ^ apart) for i in range(count)])]
    all_gather x2, waiting for transfers between devices: 71.3 us -> 0.02 us  [on_device(): lax.all_gather((filled_bands, empty_bands), 'row', axis=1, tiled=True)]
    another operation x0 -> x3, other arithmetic: none -> 15.4 us  [collected_by_bits(): both = jnp.stack([tiles, other])]
    all_gather x1, waiting for transfers between devices: 35.9 us -> 49.3 us  [on_device(): lax.all_gather(filled_bands, 'col', axis=0, tiled=True)]
    select_n x0 -> x1, other arithmetic: none -> 8.28 us  [collected_by_bits(): tiles = jnp.where(upper == 0, both, both[::-1]).reshape(-1, *shard.shape)]
  transfers between devices with their start and end apart: 6 -> 7, of which waited for: 6 -> 5; matrix products, arithmetic and copies ran while one was open for 4% -> 8% of each run, Pallas kernels for 0% -> 0%
where the time goes in v1:
time: 457 us; the launch traced here: 456 us
  waiting for transfers between devices  228 us (50%)
  blocking collectives  119 us (26%)
  matrix products  41.8 us (9%)
  local copies, waits for them, and re-layouts  27.8 us (6%)
  other arithmetic  23.7 us (5%)
  between operations  14 us (3%)
    all_to_all x1, blocking collectives, on_device(): lax.all_to_all(polar_time[None], 'tm', split_axis=2, concat_axis=0, tiled...  96.6 us
    ppermute x2, waiting for transfers between devices, collected_by_bits(): other = lax.ppermute(tiles, axis, [(i, i ^ apart) for i in range(count)])  80.8 us
    all_gather x1, waiting for transfers between devices, on_device(): lax.all_gather(empty_orbitals, 'tm', axis=2, tiled=True)  63.3 us
    all_gather x1, waiting for transfers between devices, on_device(): lax.all_gather(filled_bands, 'col', axis=0, tiled=True)  49.3 us
    all_gather x1, waiting for transfers between devices, on_device(): lax.all_gather(filled_orbitals, 'tm', axis=2, tiled=True)  33.5 us
    dot_general x2, matrix products, tile_product(): lax.dot_general(left_points.reshape(-1, band_count), scaled, (((1,), (1,)...  32.3 us
    another operation x2, local copies, waits for them, and re-layouts, on_device(): polar_time[None]  17.8 us
    another operation x3, other arithmetic, collected_by_bits(): both = jnp.stack([tiles, other])  15.4 us
  transfers between devices with their start and end apart: 7, of which 5 were waited for; matrix products, arithmetic and copies ran while one was open for 8% of the time, Pallas kernels for 0%

profile of v1, /device:TPU:0, one launch (start us, length us, event | category | flops | bytes accessed | tf_op | source)
XLA Modules:
  0.0 455.8 jit_solution(12240299391068714799)
XLA Ops:
  6.5 0.0 copy-start
  6.5 0.0 all-gather.8.cloned.1.call-start
  6.5 0.7 all-gather.8.cloned.1.call-update
  7.3 0.0 all-gather.14.cloned.1.call-start
  7.3 0.7 all-gather.14.cloned.1.call-update
  8.0 0.0 all-gather.10.cloned.1.call-start
  8.1 33.5 %all-gather.8.cloned.1.call-done = bf16[1,512,1024]{2,1,0:T(8,128)(2,1)} async-done(((bf16[1,512,256]{2,1,0:T(8,128)(2,1)}), bf16[1,512,1024]{2,1,0:T(8,128)(2,1)}) %all-gather.8.cloned.1.call-update) | async-done | bytes 1048592 | tf_op jit(solution)/shard_map/all_gather | solution.py:48
  41.6 0.0 all-gather.10.cloned.1.call-update
  41.6 0.0 all-gather.12.cloned.1.call-start
  41.7 63.3 %all-gather.14.cloned.1.call-done = bf16[1,512,3072]{2,1,0:T(8,128)(2,1)} async-done(((bf16[1,512,768]{2,1,0:T(8,128)(2,1)}), bf16[1,512,3072]{2,1,0:T(8,128)(2,1)}) %all-gather.14.cloned.1.call-update) | async-done | bytes 3145744 | tf_op jit(solution)/shard_map/all_gather | solution.py:49
  104.9 0.0 collective-permute-start
  104.9 0.0 all-gather.12.cloned.1.call-update
  105.0 0.0 all-gather.16.cloned.1.call-start
  105.0 5.8 %collective-permute-done = bf16[1,1,512,3072]{3,2,1,0:T(8,128)(2,1)S(1)} collective-permute-done((bf16[1,1,512,3072]{3,2,1,0:T(8,128)(2,1)}, bf16[1,1,512,3072]{3,2,1,0:T(8,128)(2,1)S(1)}, u32[]{:S(2)}, u32[]{:S(2)}) %collective-permute-start) | collective-permute-done | bytes 3145760 | tf_op jit(solution)/shard_map/ppermute | solution.py:18
  110.8 0.0 copy-start.1
  110.8 1.7 copy-done.1
  112.5 3.8 pad_maximum_fusion.1
  116.3 0.0 copy-start.3
  116.3 0.0 copy-start.2
  116.3 6.8 %fusion.7 = (bf16[1,2,1,512,3072]{4,3,1,2,0:T(8,128)(2,1)}, bf16[2,1,512,3072]{3,2,0,1:T(8,128)(2,1)}) fusion(bf16[2,1,1,512,3072]{4,3,2,1,0:T(8,128)(2,1)S(1)} %pad_maximum_fusion.1, pred[]{:T(512)S(6)} %eq.7), kind=kLoop, calls=%fused_computation.13 | loop fusion | flops 3145728 | bytes 18874368 | tf_op jit(solution)/shard_map/stack;reshape | solution.py:19
  123.1 1.5 collective-permute-start.1
  124.6 0.0 slice-start
  124.6 0.0 all-gather.16.cloned.1.call-update
  125.5 0.0 copy-done.3
  125.5 0.0 copy-done.2
  125.5 8.6 %all-gather = bf16[4,1,256]{2,1,0:T(2,128)(2,1)S(1)} all-gather(bf16[1,1,256]{2,1,0:T(2,128)(2,1)S(1)} %reshape.26), channel_id=1, replica_groups=mesh['row'=2,'col'=4,'tm'=4] {'tm'}, dimensions={0}, use_global_device_ids=true | all-gather | bytes 2560 | tf_op jit(solution)/shard_map/all_gather | solution.py:50
  134.1 13.3 %all-gather.1 = bf16[4,1,768]{2,1,0:T(2,128)(2,1)S(1)} all-gather(bf16[1,1,768]{2,1,0:T(2,128)(2,1)S(1)} %reshape.28), channel_id=1, replica_groups=mesh['row'=2,'col'=4,'tm'=4] {'tm'}, dimensions={0}, use_global_device_ids=true | all-gather | bytes 7680 | tf_op jit(solution)/shard_map/all_gather | solution.py:51
  147.4 0.0 all-gather.10.cloned.1.call-done
  147.5 49.3 %all-gather.12.cloned.1.call-done = bf16[4,512,1024]{2,1,0:T(8,128)(2,1)} async-done(((bf16[1,512,1024]{2,1,0:T(8,128)(2,1)}), bf16[4,512,1024]{2,1,0:T(8,128)(2,1)}) %all-gather.12.cloned.1.call-update) | async-done | bytes 4194320 | tf_op jit(solution)/shard_map/all_gather | solution.py:54
  196.7 0.0 slice-start.1
  196.7 11.7 %fusion.13 = f32[1024,2048]{1,0:T(8,128)} fusion(bf16[2048,1024]{1,0:T(8,128)(2,1)} %bitcast.55, bf16[1,1024,1024]{2,1,0:T(8,128)(2,1)} %all-gather.10.cloned.1.call-done, f32[1024]{0:T(1024)S(1)} %bitcast.54), kind=kOutput, calls=%fused_computation.18 | convolution fusion | flops 4298113024 | bytes 14684160 | tf_op jit(solution)/shard_map/dot_general | solution.py:35
  208.4 75.0 %collective-permute-done.1 = bf16[2,1,512,3072]{3,2,0,1:T(8,128)(2,1)} collective-permute-done((bf16[2,1,512,3072]{3,2,0,1:T(8,128)(2,1)}, bf16[2,1,512,3072]{3,2,0,1:T(8,128)(2,1)}, u32[]{:S(2)}, u32[]{:S(2)}) %collective-permute-start.1) | collective-permute-done | bytes 6291488 | tf_op jit(solution)/shard_map/ppermute | solution.py:18
  283.5 0.0 slice-done
  283.5 0.0 slice-done.1
  283.5 4.8 %pad_maximum_fusion = bf16[2,2,1,512,3072]{4,3,1,2,0:T(8,128)(2,1)S(1)} fusion(bf16[1,2,1,512,3072]{4,3,1,2,0:T(8,128)(2,1)} %bitcast.10, bf16[1,2,1,512,3072]{4,3,1,2,0:T(8,128)(2,1)S(1)} %bitcast.47), kind=kLoop, calls=%fused_computation.1 | loop fusion | flops 6291456 | bytes 25165824 | tf_op jit(solution)/shard_map/stack | solution.py:19
  288.2 8.3 %reverse_select_fusion = bf16[2,2,1,512,3072]{4,3,1,2,0:T(8,128)(2,1)} fusion(bf16[2,2,1,512,3072]{4,3,1,2,0:T(8,128)(2,1)S(1)} %pad_maximum_fusion, pred[]{:T(512)S(6)} %eq.6), kind=kLoop, calls=%fused_computation | loop fusion | flops 6291456 | bytes 25165824 | tf_op jit(solution)/shard_map/jit(_where)/select_n | solution.py:21
  296.5 0.0 all-gather.16.cloned.1.call-done
  296.5 20.6 %fusion.1 = bf16[2048,1024]{0,1:T(8,128)(2,1)} fusion(f32[1024,2048]{1,0:T(8,128)} %fusion.13, bf16[2048,3072]{1,0:T(8,128)(2,1)} %bitcast.51, bf16[1,1024,3072]{2,1,0:T(8,128)(2,1)} %all-gather.16.cloned.1.call-done, f32[3072]{0:T(1024)S(1)} %bitcast.53), kind=kOutput, calls=%fused_computation.6 | convolution fusion | flops 12900630528 | bytes 31469568 | tf_op jit(solution)/shard_map/dot_general | solution.py:35
  317.1 7.8 %broadcast_in_dim_reshape.3 = bf16[1,4,512,1024]{2,1,3,0:T(4,128)(2,1)} reshape(bf16[2048,1024]{0,1:T(8,128)(2,1)} %fusion.1) | data formatting | bytes 8388608 | tf_op jit(solution)/shard_map/broadcast_in_dim;reshape | solution.py:70
  324.9 10.0 %copy.14 = bf16[1,4,512,1024]{3,1,0,2:T(4,128)(2,1)} copy(bf16[1,4,512,1024]{2,1,3,0:T(4,128)(2,1)} %broadcast_in_dim_reshape.3) | data formatting | bytes 8388608 | tf_op jit(solution)/shard_map/broadcast_in_dim;reshape | solution.py:70
  335.0 96.6 %all_to_all.18 = bf16[1,4,512,1024]{3,1,0,2:T(4,128)(2,1)S(1)} all-to-all(bf16[1,4,512,1024]{3,1,0,2:T(4,128)(2,1)} %copy.14), channel_id=1, replica_groups=mesh['row'=2,'col'=4,'tm'=4] {'tm'}, dimensions={2} | all-to-all | bytes 8388608 | tf_op jit(solution)/shard_map/all_to_all | solution.py:70
  431.6 0.0 copy-done
  431.6 9.4 %convolution_bitcast_fusion = f32[4,4,128,1024]{3,0,2,1:T(4,128)S(1)} fusion(bf16[1,4,4,128,1024]{4,1,3,2,0:T(4,128)(2,1)S(1)} %bitcast.48, f32[4,4]{1,0:T(4,128)S(1)} %copy-done), kind=kOutput, calls=%fused_computation.11 | convolution fusion | flops 100663296 | bytes 12582976 | tf_op jit(solution)/shard_map/ft,tabc->fabc/dot_general | solution.py:67
  441.1 8.3 %copy.17 = f32[4,4,128,1024]{3,2,1,0:T(8,128)} copy(f32[4,4,128,1024]{3,0,2,1:T(4,128)S(1)} %convolution_bitcast_fusion) | data formatting | bytes 16777216 | tf_op jit(solution)/shard_map/ft,tabc->fabc/dot_general | solution.py:67
  (5 shorter events, 0.1 us)
Async XLA Ops:
  6.5 425.1 %copy-start = (f32[4,4]{1,0:T(4,128)S(1)}, f32[4,4]{1,0:T(4,128)}, u32[]{:S(2)}) copy-start(f32[4,4]{1,0:T(4,128)} %param.11) | copy-start | bytes 196
  6.5 35.0 %all-gather.8.cloned.1.call-start = ((), (), s32[]{:S(2)}) async-start(), calls=%async_computation.1 | async-start | bytes 1310720 | tf_op jit(solution)/shard_map/all_gather | solution.py:48
  7.3 97.7 %all-gather.14.cloned.1.call-start = ((), (), s32[]{:S(2)}) async-start(), calls=%async_computation.4 | async-start | bytes 3932160 | tf_op jit(solution)/shard_map/all_gather | solution.py:49
  8.0 139.4 %all-gather.10.cloned.1.call-start = ((), (), s32[]{:S(2)}) async-start(), calls=%async_computation.2 | async-start | bytes 3145728 | tf_op jit(solution)/shard_map/all_gather | solution.py:57
  41.6 155.1 %all-gather.12.cloned.1.call-start = ((), (), s32[]{:S(2)}) async-start(), calls=%async_computation.3 | async-start | bytes 5242880 | tf_op jit(solution)/shard_map/all_gather | solution.py:54
  104.9 5.9 %collective-permute-start = (bf16[1,1,512,3072]{3,2,1,0:T(8,128)(2,1)}, bf16[1,1,512,3072]{3,2,1,0:T(8,128)(2,1)S(1)}, u32[]{:S(2)}, u32[]{:S(2)}) collective-permute-start(bf16[1,1,512,3072]{3,2,1,0:T(8,128)(2,1)} %bitcast.49), channel_id=1, source_target_pairs={{0,4},{4,0},{8,12},{12,8},{1,5},{5,1},{9,13},{13,9},{2,6},{6,2},{1... | collective-permute-start | bytes 9437192 | tf_op jit(solution)/shard_map/ppermute | solution.py:18
  105.0 191.6 %all-gather.16.cloned.1.call-start = ((), (), s32[]{:S(2)}) async-start(), calls=%async_computation.5 | async-start | bytes 9437184 | tf_op jit(solution)/shard_map/all_gather | solution.py:57
  110.8 1.7 copy-start.1
  116.3 9.1 %copy-start.3 = (bf16[256]{0:T(256)(128)(2,1)S(1)}, bf16[256]{0:T(256)(128)(2,1)}, u32[]{:S(2)}) copy-start(bf16[256]{0:T(256)(128)(2,1)} %param.8) | copy-start | bytes 1540
  116.3 9.2 %copy-start.2 = (bf16[768]{0:T(1024)(128)(2,1)S(1)}, bf16[768]{0:T(1024)(128)(2,1)}, u32[]{:S(2)}) copy-start(bf16[768]{0:T(1024)(128)(2,1)} %param.9) | copy-start | bytes 4612
  123.1 160.4 %collective-permute-start.1 = (bf16[2,1,512,3072]{3,2,0,1:T(8,128)(2,1)}, bf16[2,1,512,3072]{3,2,0,1:T(8,128)(2,1)}, u32[]{:S(2)}, u32[]{:S(2)}) collective-permute-start(bf16[2,1,512,3072]{3,2,0,1:T(8,128)(2,1)} %get-tuple-element.6), channel_id=1, source_target_pairs={{0,8},{4,12},{8,0},{12,4},{1,9},{5,13},{9,1},{13,5},{2,10},{6,14},... | collective-permute-start | bytes 18874376 | tf_op jit(solution)/shard_map/ppermute | solution.py:18
  124.6 158.9 %slice-start = ((s8[6291456]{0:T(1024)(128)(4,1)}), s8[2097152]{0:T(1024)(128)(4,1)S(1)}, s32[]{:S(2)}) async-start(s8[6291456]{0:T(1024)(128)(4,1)} %bitcast.46), calls=%async_computation.6 | async-start | bytes 4194304
  196.7 86.8 %slice-start.1 = ((s8[6291456]{0:T(1024)(128)(4,1)}), s8[4194304]{0:T(1024)(128)(4,1)S(1)}, s32[]{:S(2)}) async-start(s8[6291456]{0:T(1024)(128)(4,1)} %bitcast.46), calls=%async_computation.7 | async-start | bytes 8388608
Sparse Core Ops, SparseCore 0:
  8.9 32.6 all-gather.7
  43.1 61.7 all-gather.13
  106.5 31.7 all-gather.9
  139.7 57.0 all-gather.11
  198.1 80.3 all-gather.15
